TPU v7x, 256 devices: a whole 4x4x8 slice. The times are simulated.
256 devices in a mesh: src: 16 (over x_lo, y, core), rcv: 16 (over z, x_hi).
Axes of the slice: x: 4 (x_hi: 2, x_lo: 2; x = x_hi * 2 + x_lo), y: 4, z: 8, core: 2. Of those that a mesh axis runs over, the one named last changes fastest.
Arguments:
- recorded: bfloat16 [2, 16384, 16384], P(None, 'src', 'rcv'), may hold values from -6 to 6
- obliquity: float32 [16, 1024], replicated, may hold values from 0.01 to 0.25
- clip_level: float32 [16384], P('src'), may hold values from 0.3 to 3
Outputs:
- first_pass: bfloat16 [2, 16384, 16384], P(None, 'src', 'rcv')
- primaries: bfloat16 [2, 16384, 16384], P(None, 'src', 'rcv')
All inputs are finite; a program needn't handle non-finite values.
Results may differ from a plain program's by a relative error of at most 0.0025.
Values may be sent and summed in bfloat16 or wider, within the bound.
A program may use at most 128 MiB of HBM per device.

v0:
```python
import math
import jax
import jax.numpy as jnp
from jax import lax
from jax.sharding import PartitionSpec as P

N = 16384
K = 256
TWO_PI = 2.0 * math.pi


def rotate(real_part, imag_part, cosine, sine_part):
    return (real_part * cosine - imag_part * sine_part, real_part * sine_part + imag_part * cosine)


def twiddle(real_part, imag_part, column_index, group_index, orient, total_length):
    angles = (column_index * group_index % total_length).astype(jnp.float32) * (
        TWO_PI / total_length
    )
    return rotate(real_part, imag_part, jnp.cos(angles), orient * jnp.sin(angles))


def long_table(length, orient):
    index_left = lax.broadcasted_iota(jnp.int32, (length, length), 0)
    index_right = lax.broadcasted_iota(jnp.int32, (length, length), 1)
    angles = (index_left * index_right % length).astype(jnp.float32) * (TWO_PI / length)
    cosine = jnp.cos(angles)
    sine_part = orient * jnp.sin(angles)
    upper = jnp.concatenate([cosine, sine_part], axis=1)
    lower = jnp.concatenate([-sine_part, cosine], axis=1)
    return jnp.concatenate([upper, lower], axis=0)


def long_transform(real_part, imag_part, orient):
    length = real_part.shape[-1]
    joined = jnp.concatenate([real_part, imag_part], axis=-1)
    result = jnp.dot(
        joined.reshape(-1, 2 * length),
        long_table(length, orient),
        precision=lax.Precision.HIGHEST,
        preferred_element_type=jnp.float32,
    )
    result = result.reshape(joined.shape)
    return (result[..., :length], result[..., length:])


def across_groups(real_part, imag_part, groups, orient):
    index_left = lax.broadcasted_iota(jnp.int32, (groups, groups), 0)
    index_right = lax.broadcasted_iota(jnp.int32, (groups, groups), 1)
    angles = (index_left * index_right % groups).astype(jnp.float32) * (TWO_PI / groups)
    cosine = jnp.cos(angles)
    sine_part = orient * jnp.sin(angles)
    highest = lax.Precision.HIGHEST
    new_real = jnp.einsum("mgc,gk->mkc", real_part, cosine, precision=highest) - jnp.einsum(
        "mgc,gk->mkc", imag_part, sine_part, precision=highest
    )
    new_imag = jnp.einsum("mgc,gk->mkc", real_part, sine_part, precision=highest) + jnp.einsum(
        "mgc,gk->mkc", imag_part, cosine, precision=highest
    )
    return (new_real, new_imag)


def filter_rows(whole_rows, obliquity, groups):
    row_total = whole_rows.shape[1]
    group_cols = whole_rows.shape[2] // groups
    total_length = groups * group_cols
    values = whole_rows.astype(jnp.float32).reshape(2, row_total, groups, group_cols)
    real_part, imag_part = across_groups(values[0], values[1], groups, -1.0)
    column_index = lax.broadcasted_iota(jnp.int32, (1, 1, group_cols), 2)
    group_index = lax.broadcasted_iota(jnp.int32, (1, groups, 1), 1)
    real_part, imag_part = twiddle(
        real_part, imag_part, column_index, group_index, -1.0, total_length
    )
    real_part, imag_part = long_transform(real_part, imag_part, -1.0)
    real_part = real_part * obliquity[None]
    imag_part = imag_part * obliquity[None]
    real_part, imag_part = long_transform(real_part, imag_part, 1.0)
    real_part, imag_part = twiddle(
        real_part, imag_part, column_index, group_index, 1.0, total_length
    )
    real_part, imag_part = across_groups(real_part, imag_part, groups, 1.0)
    inverse_scale = 1.0 / total_length
    returned = jnp.stack([real_part * inverse_scale, imag_part * inverse_scale])
    return returned.reshape(2, row_total, total_length).astype(jnp.bfloat16)


def through_rows(panel_rows, obliquity):
    moved_rows = lax.all_to_all(panel_rows, "rcv", split_axis=1, concat_axis=2, tiled=True)
    returned = filter_rows(moved_rows, obliquity, lax.axis_size("rcv"))
    return lax.all_to_all(returned, "rcv", split_axis=2, concat_axis=1, tiled=True)


def complex_product(left_rows, right_rows):
    left_joined = jnp.concatenate([left_rows[0], left_rows[1]], axis=0)
    upper = jnp.concatenate([right_rows[0], right_rows[1]], axis=1)
    lower = jnp.concatenate([-right_rows[1], right_rows[0]], axis=1)
    right_joined = jnp.concatenate([upper, lower], axis=0)
    return lax.dot_general(
        left_joined, right_joined, (((0,), (0,)), ((), ())), preferred_element_type=jnp.float32
    )


def per_device(recorded, obliquity, clip_level):
    spacing = N // K
    row_total = recorded.shape[1]
    col_total = recorded.shape[2]
    panel_rows = recorded.reshape(2, row_total // spacing, spacing, col_total)[:, :, 0, :]
    filtered = through_rows(panel_rows, obliquity)
    clip_rows = clip_level[:, None]
    estimate = recorded
    passes = []
    for update_index in range(2):
        columns = estimate.reshape(2, row_total, col_total // spacing, spacing)[:, :, :, 0]
        left_local = jnp.swapaxes(columns, 1, 2)
        left_panel = lax.all_gather(left_local, "rcv", axis=1, tiled=True)

        def accumulate(running, panel_piece, first_row, left_all=left_panel):
            return complex_product(left_all, panel_piece)

        zeros_init = jnp.zeros((row_total, 2 * col_total), jnp.float32)
        product_sum = accumulate(
            zeros_init, lax.all_gather(filtered, "src", axis=1, tiled=True), jnp.int32(0)
        )
        pred_real = product_sum[:, :col_total]
        pred_imag = product_sum[:, col_total:]
        limiter = lax.rsqrt(
            1.0 + (pred_real * pred_real + pred_imag * pred_imag) / (clip_rows * clip_rows)
        )
        estimate = (
            recorded.astype(jnp.float32) - jnp.stack([pred_real * limiter, pred_imag * limiter])
        ).astype(jnp.bfloat16)
        passes.append(estimate)
    return (passes[0], passes[1])


def solution(mesh):
    return jax.shard_map(
        per_device,
        mesh=mesh,
        in_specs=(P(None, "src", "rcv"), P(), P("src")),
        out_specs=(P(None, "src", "rcv"), P(None, "src", "rcv")),
        check_vma=False,
    )
```

profile of v0, /device:TPU:8, one launch (start us, length us, event | category | flops | bytes accessed | tf_op | source)
XLA Modules:
  0.0 447.1 jit_solution(7777668069207956827)
XLA Ops:
  7.2 1.1 slice.88
  8.3 0.7 copy.65
  9.0 11.0 %all-to-all-start = ((bf16[2,16,1024]{2,0,1:T(2,128)(2,1)}), bf16[2,16,1024]{2,0,1:T(2,128)(2,1)S(1)}, u32[]{:S(2)}, u32[]{:S(2)}) async-start(bf16[2,16,1024]{2,0,1:T(2,128)(2,1)} %bitcast.83), calls=%async_computation | async-start | bytes 131072 | tf_op jit(solution)/shard_map/all_to_all | solution.py:88
  20.1 6.2 %copy.36 = bf16[2,1024,1024]{1,2,0:T(8,128)(2,1)} copy(bf16[2,1024,1024]{2,1,0:T(8,128)(2,1)} %param.3) | data formatting | bytes 8388608 | tf_op args[0]
  26.3 1.1 slice.85
  28.2 17.6 %broadcast_multiply_fusion = (f32[1024,1024]{1,0:T(8,128)}, f32[1024,1024]{1,0:T(8,128)}) fusion(), kind=kLoop, calls=%fused_computation.35 | loop fusion | flops 15728640 | bytes 8388608 | tf_op jit(solution)/shard_map/mul | solution.py:28
  45.8 16.3 %fusion.27 = f32[1024,1024]{1,0:T(8,128)} fusion(), kind=kLoop, calls=%fused_computation.39 | loop fusion | flops 16777216 | bytes 4194304 | tf_op jit(solution)/shard_map/neg | solution.py:30
  62.1 16.7 %fusion.24 = (f32[1024,1024]{1,0:T(8,128)}, f32[1024,1024]{1,0:T(8,128)}) fusion(), kind=kLoop, calls=%fused_computation.36 | loop fusion | flops 15728640 | bytes 8388608 | tf_op jit(solution)/shard_map/sin | solution.py:28
  80.3 13.8 %fusion.21 = f32[1,16,2048]{2,1,0:T(8,128)S(1)} fusion(f32[1024,1024]{1,0:T(8,128)} %get-tuple-element.19, f32[1024,1024]{1,0:T(8,128)} %fusion.27, f32[1024,1024]{1,0:T(8,128)} %get-tuple-element.18, f32[1,16,1024]{2,1,0:T(8,128)S(1)} %get-tuple-element.15, f32[1,16,1024]{2,1,0:T(8,128)S(1)} %get-tuple-element.14), kind=kOutput, calls=%fused_computation.33 | convolution fusion | flops 817922048 | bytes 12845056 | tf_op jit(solution)/shard_map/dot_general | solution.py:37
  94.2 14.0 %fusion.18 = f32[1,16,2048]{2,1,0:T(8,128)S(1)} fusion(f32[1024,1024]{1,0:T(8,128)} %get-tuple-element.19, f32[1024,1024]{1,0:T(8,128)} %get-tuple-element.21, f32[1024,1024]{1,0:T(8,128)} %get-tuple-element.20, f32[1,16,1024]{2,1,0:T(8,128)S(1)} %get-tuple-element.13, f32[1,16,1024]{2,1,0:T(8,128)S(1)} %get-tuple-element.12), kind=kOutput, calls=%fused_computation.32 | convolution fusion | flops 817922048 | bytes 12845056 | tf_op jit(solution)/shard_map/dot_general | solution.py:37
  109.7 11.5 %stack.36 = bf16[1,1,16384]{0,1,2:T(2,128)(2,1)} reshape(bf16[16,1024]{1,0:T(8,128)(2,1)S(1)} %fusion.30) | data formatting | bytes 65536 | tf_op jit(solution)/shard_map/stack | solution.py:83
  121.7 12.0 %stack.37 = bf16[1,1,16384]{0,1,2:T(2,128)(2,1)} reshape(bf16[16,1024]{1,0:T(8,128)(2,1)S(1)} %fusion.31) | data formatting | bytes 65536 | tf_op jit(solution)/shard_map/stack | solution.py:83
  133.6 25.2 %fusion.139 = bf16[16384,1,2]{2,1,0:T(2,128)(2,1)} fusion(bf16[1,1,16384]{0,1,2:T(2,128)(2,1)} %stack.37, bf16[1,1,16384]{0,1,2:T(2,128)(2,1)} %stack.36), kind=kLoop, calls=%fused_computation.177 | loop fusion | flops 131072 | bytes 131072
  159.4 90.8 %reduce = bf16[16384,2]{1,0:T(8,128)(2,1)} reduce(bf16[16384,1,2]{2,1,0:T(2,128)(2,1)} %fusion.139, bf16[]{:T(256)} %broadcast.277), dimensions={1}, to_apply=%fusion.139.reduce_sub_computation | reduce | bytes 131074
  250.2 7.2 %reshape.220 = bf16[16,2,1024]{2,1,0:T(2,128)(2,1)S(1)} reshape(bf16[16384,2]{1,0:T(8,128)(2,1)} %reduce) | data formatting | bytes 131072
  257.3 20.0 %all_to_all.21 = bf16[16,2,1024]{2,1,0:T(2,128)(2,1)S(1)} all-to-all(bf16[16,2,1024]{2,1,0:T(2,128)(2,1)S(1)} %reshape.220), channel_id=1, replica_groups=mesh['src'=16,'rcv'=16] {'rcv'}, dimensions={0} | all-to-all | bytes 131072 | tf_op jit(solution)/shard_map/all_to_all | solution.py:90
  277.3 11.9 %reshape.221 = bf16[16384,1,2]{2,1,0:T(2,128)(2,1)} reshape(bf16[16,2,1024]{2,1,0:T(2,128)(2,1)S(1)} %all_to_all.21) | data formatting | bytes 131072
  289.2 15.4 %copy.42 = bf16[2,1,16384]{2,0,1:T(2,128)(2,1)S(1)} copy(bf16[2,1,16384]{0,1,2:T(2,128)(2,1)} %bitcast.85) | data formatting | bytes 131072 | tf_op jit(solution)/shard_map/all_to_all | solution.py:90
  305.5 1.3 slice_bitcast_fusion.5
  306.8 26.9 %all-gather.6.cloned.1.call-done = bf16[2,256,1024]{2,1,0:T(8,128)(2,1)} async-done(((bf16[2,16,1024]{2,1,0:T(8,128)(2,1)}), bf16[2,256,1024]{2,1,0:T(8,128)(2,1)}) %all-gather.6.cloned.1.call-update) | async-done | bytes 1048592 | tf_op jit(solution)/shard_map/all_gather | solution.py:122
  333.7 1.3 slice_bitcast_fusion.2
  335.0 1.1 fusion.137
  336.1 2.4 fusion.32
  338.5 2.4 multiply_bitcast_fusion.3
  340.9 3.0 fusion.10
  343.9 6.2 %copy.43 = bf16[2,1024,1024]{1,2,0:T(8,128)(2,1)} copy(bf16[2,1024,1024]{2,1,0:T(8,128)(2,1)} %fusion.10) | data formatting | bytes 8388608 | tf_op jit(solution)/shard_map/convert_element_type | solution.py:131
  350.1 1.1 slice.99
  351.9 79.3 %all-gather.8.cloned.1.call-done = bf16[2,256,1024]{2,1,0:T(8,128)(2,1)} async-done(((bf16[2,16,1024]{2,1,0:T(8,128)(2,1)}), bf16[2,256,1024]{2,1,0:T(8,128)(2,1)}) %all-gather.8.cloned.1.call-update) | async-done | bytes 1048592 | tf_op jit(solution)/shard_map/all_gather | solution.py:115
  431.3 1.3 slice_bitcast_fusion.1
  432.5 2.4 fusion.36
  435.0 2.4 multiply_bitcast_fusion.1
  437.4 3.0 fusion.11
  (31 shorter events, 6.2 us)
Async XLA Ops:
  9.0 69.8 %all-to-all-start = ((bf16[2,16,1024]{2,0,1:T(2,128)(2,1)}), bf16[2,16,1024]{2,0,1:T(2,128)(2,1)S(1)}, u32[]{:S(2)}, u32[]{:S(2)}) async-start(bf16[2,16,1024]{2,0,1:T(2,128)(2,1)} %bitcast.83), calls=%async_computation | async-start | bytes 131072 | tf_op jit(solution)/shard_map/all_to_all | solution.py:88
  20.1 285.5 %all-gather.4.cloned.1.call-start = ((), (), s32[]{:S(2)}) async-start(), calls=%async_computation.2 | async-start | bytes 1114112 | tf_op jit(solution)/shard_map/all_gather | solution.py:115
  28.1 305.6 %all-gather.6.cloned.1.call-start = ((), (), s32[]{:S(2)}) async-start(), calls=%async_computation.3 | async-start | bytes 1114112 | tf_op jit(solution)/shard_map/all_gather | solution.py:122
  80.3 13.9 %copy-start.2 = (f32[16,1024]{1,0:T(8,128)S(1)}, f32[16,1024]{1,0:T(8,128)}, u32[]{:S(2)}) copy-start(f32[16,1024]{1,0:T(8,128)} %param.4) | copy-start | bytes 196612
  289.2 16.3 %copy-start.3 = (f32[1024]{0:T(1024)S(1)}, f32[1024]{0:T(1024)}, u32[]{:S(2)}) copy-start(f32[1024]{0:T(1024)} %param.5) | copy-start | bytes 12292
  305.3 126.0 %all-gather.8.cloned.1.call-start = ((), (), s32[]{:S(2)}) async-start(), calls=%async_computation.4 | async-start | bytes 1114112 | tf_op jit(solution)/shard_map/all_gather | solution.py:115
  338.5 2.5 copy-start
  434.9 2.5 copy-start.1
Sparse Core Ops, SparseCore 0:
  28.2 80.2 all-gather.3
  305.4 28.2 all-gather.5
  352.0 79.1 all-gather.7
where the time goes:
time: 452 us; the launch traced here: 447 us
  other arithmetic  179 us (40%)
  waiting for transfers between devices  106 us (23%)
  local copies, waits for them, and re-layouts  80.7 us (18%)
  matrix products  35.9 us (8%)
  blocking collectives  20 us (4%)
  between operations  14.2 us (3%)
  starting transfers between devices  11.3 us (2%)
    unnamed x2, other arithmetic  116 us
    all_gather x2, waiting for transfers between devices, per_device(): left_panel = lax.all_gather(left_local, 'rcv', axis=1, tiled=True)  79.4 us
    dot_general x2, matrix products, long_transform(): jnp.dot(joined.reshape(-1, 2 * length), long_table(length, orient), preci...  27.9 us
    unnamed x15, local copies, waits for them, and re-layouts  27.8 us
    all_gather x1, waiting for transfers between devices, per_device(): lax.all_gather(filtered, 'src', axis=1, tiled=True)  26.9 us
    another operation x2, local copies, waits for them, and re-layouts, filter_rows(): returned = jnp.stack([real_part * inverse_scale, imag_part * inverse_scale])  23.4 us
    all_to_all x1, blocking collectives, through_rows(): lax.all_to_all(returned, 'rcv', split_axis=2, concat_axis=1, tiled=True)  20 us
    mul x1, other arithmetic, long_table(): sine_part = orient * jnp.sin(angles)  17.6 us
  transfers between devices with their start and end apart: 4, of which 2 were waited for; matrix products, arithmetic and copies ran while one was open for 60% of the time, Pallas kernels for 0%

commit v1 on v0

--- a/solution.py
+++ b/solution.py
@@ -119,7 +119,14 @@
 
         zeros_init = jnp.zeros((row_total, 2 * col_total), jnp.float32)
         product_sum = accumulate(
-            zeros_init, lax.all_gather(filtered, "src", axis=1, tiled=True), jnp.int32(0)
+            zeros_init,
+            jnp.concatenate(
+                lax.all_to_all(
+                    jnp.stack([filtered for _ in range(lax.axis_size("src"))]), "src", 0, 0
+                ),
+                1,
+            ),
+            jnp.int32(0),
         )
         pred_real = product_sum[:, :col_total]
         pred_imag = product_sum[:, col_total:]

time: 452 us -> 437 us (0.967)
  waiting for transfers between devices: 106 us -> 87.7 us
  starting transfers between devices: 11.3 us -> 16.2 us
    all_gather x1 -> x0, waiting for transfers between devices: 26.9 us -> none  [per_device(): lax.all_gather(filtered, 'src', axis=1, tiled=True)]
    all_to_all x0 -> x1, waiting for transfers between devices: none -> 13.3 us  [per_device(): lax.all_to_all(jnp.stack([filtered for _ in range(lax.axis_size('src'))])...]
    all_to_all x0 -> x1, starting transfers between devices: none -> 5.12 us  [per_device(): lax.all_to_all(jnp.stack([filtered for _ in range(lax.axis_size('src'))])...]
    all_gather x2, waiting for transfers between devices: 79.4 us -> 74.4 us  [per_device(): left_panel = lax.all_gather(left_local, 'rcv', axis=1, tiled=True)]
  transfers between devices with their start and end apart: 4 -> 4, of which waited for: 2 -> 2; matrix products, arithmetic and copies ran while one was open for 60% -> 61% of each run, Pallas kernels for 0% -> 0%
where the time goes in v1:
time: 437 us; the launch traced here: 432 us
  other arithmetic  178 us (41%)
  waiting for transfers between devices  87.7 us (20%)
  local copies, waits for them, and re-layouts  80 us (18%)
  matrix products  35.9 us (8%)
  blocking collectives  20 us (5%)
  starting transfers between devices  16.2 us (4%)
  between operations  14.5 us (3%)
    unnamed x2, other arithmetic  116 us
    all_gather x2, waiting for transfers between devices, per_device(): left_panel = lax.all_gather(left_local, 'rcv', axis=1, tiled=True)  74.4 us
    dot_general x2, matrix products, long_transform(): jnp.dot(joined.reshape(-1, 2 * length), long_table(length, orient), preci...  27.9 us
    unnamed x15, local copies, waits for them, and re-layouts  27.1 us
    another operation x2, local copies, waits for them, and re-layouts, filter_rows(): returned = jnp.stack([real_part * inverse_scale, imag_part * inverse_scale])  23.4 us
    all_to_all x1, blocking collectives, through_rows(): lax.all_to_all(returned, 'rcv', split_axis=2, concat_axis=1, tiled=True)  20 us
    mul x1, other arithmetic, long_table(): sine_part = orient * jnp.sin(angles)  17.6 us
    sin x1, other arithmetic, long_table(): sine_part = orient * jnp.sin(angles)  16.7 us
  transfers between devices with their start and end apart: 4, of which 2 were waited for; matrix products, arithmetic and copies ran while one was open for 61% of the time, Pallas kernels for 0%

profile of v1, /device:TPU:8, one launch (start us, length us, event | category | flops | bytes accessed | tf_op | source)
XLA Modules:
  0.0 432.0 jit_solution(10069409558429624840)
XLA Ops:
  7.2 1.1 slice.90
  8.3 0.7 copy.65
  9.0 11.0 %all-to-all-start = ((bf16[2,16,1024]{2,0,1:T(2,128)(2,1)}), bf16[2,16,1024]{2,0,1:T(2,128)(2,1)S(1)}, u32[]{:S(2)}, u32[]{:S(2)}) async-start(bf16[2,16,1024]{2,0,1:T(2,128)(2,1)} %bitcast.81), calls=%async_computation | async-start | bytes 131072 | tf_op jit(solution)/shard_map/all_to_all | solution.py:88
  20.1 6.2 %copy.36 = bf16[2,1024,1024]{1,2,0:T(8,128)(2,1)} copy(bf16[2,1024,1024]{2,1,0:T(8,128)(2,1)} %param.3) | data formatting | bytes 8388608 | tf_op args[0]
  26.3 1.1 slice.87
  28.1 17.6 %broadcast_multiply_fusion = (f32[1024,1024]{1,0:T(8,128)}, f32[1024,1024]{1,0:T(8,128)}) fusion(), kind=kLoop, calls=%fused_computation.35 | loop fusion | flops 15728640 | bytes 8388608 | tf_op jit(solution)/shard_map/mul | solution.py:28
  45.7 16.3 %fusion.27 = f32[1024,1024]{1,0:T(8,128)} fusion(), kind=kLoop, calls=%fused_computation.39 | loop fusion | flops 16777216 | bytes 4194304 | tf_op jit(solution)/shard_map/neg | solution.py:30
  62.1 16.7 %fusion.24 = (f32[1024,1024]{1,0:T(8,128)}, f32[1024,1024]{1,0:T(8,128)}) fusion(), kind=kLoop, calls=%fused_computation.36 | loop fusion | flops 15728640 | bytes 8388608 | tf_op jit(solution)/shard_map/sin | solution.py:28
  80.2 13.8 %fusion.21 = f32[1,16,2048]{2,1,0:T(8,128)S(1)} fusion(f32[1024,1024]{1,0:T(8,128)} %get-tuple-element.19, f32[1024,1024]{1,0:T(8,128)} %fusion.27, f32[1024,1024]{1,0:T(8,128)} %get-tuple-element.18, f32[1,16,1024]{2,1,0:T(8,128)S(1)} %get-tuple-element.15, f32[1,16,1024]{2,1,0:T(8,128)S(1)} %get-tuple-element.14), kind=kOutput, calls=%fused_computation.33 | convolution fusion | flops 817922048 | bytes 12845056 | tf_op jit(solution)/shard_map/dot_general | solution.py:37
  94.1 14.0 %fusion.18 = f32[1,16,2048]{2,1,0:T(8,128)S(1)} fusion(f32[1024,1024]{1,0:T(8,128)} %get-tuple-element.19, f32[1024,1024]{1,0:T(8,128)} %get-tuple-element.21, f32[1024,1024]{1,0:T(8,128)} %get-tuple-element.20, f32[1,16,1024]{2,1,0:T(8,128)S(1)} %get-tuple-element.13, f32[1,16,1024]{2,1,0:T(8,128)S(1)} %get-tuple-element.12), kind=kOutput, calls=%fused_computation.32 | convolution fusion | flops 817922048 | bytes 12845056 | tf_op jit(solution)/shard_map/dot_general | solution.py:37
  109.6 11.5 %stack.33 = bf16[1,1,16384]{0,1,2:T(2,128)(2,1)} reshape(bf16[16,1024]{1,0:T(8,128)(2,1)S(1)} %fusion.30) | data formatting | bytes 65536 | tf_op jit(solution)/shard_map/stack | solution.py:83
  121.6 11.9 %stack.34 = bf16[1,1,16384]{0,1,2:T(2,128)(2,1)} reshape(bf16[16,1024]{1,0:T(8,128)(2,1)S(1)} %fusion.31) | data formatting | bytes 65536 | tf_op jit(solution)/shard_map/stack | solution.py:83
  133.5 25.2 %fusion.139 = bf16[16384,1,2]{2,1,0:T(2,128)(2,1)} fusion(bf16[1,1,16384]{0,1,2:T(2,128)(2,1)} %stack.34, bf16[1,1,16384]{0,1,2:T(2,128)(2,1)} %stack.33), kind=kLoop, calls=%fused_computation.176 | loop fusion | flops 131072 | bytes 131072
  159.3 90.8 %reduce = bf16[16384,2]{1,0:T(8,128)(2,1)} reduce(bf16[16384,1,2]{2,1,0:T(2,128)(2,1)} %fusion.139, bf16[]{:T(256)} %broadcast.278), dimensions={1}, to_apply=%fusion.139.reduce_sub_computation | reduce | bytes 131074
  250.1 7.2 %reshape.234 = bf16[16,2,1024]{2,1,0:T(2,128)(2,1)S(1)} reshape(bf16[16384,2]{1,0:T(8,128)(2,1)} %reduce) | data formatting | bytes 131072
  257.3 20.0 %all_to_all.24 = bf16[16,2,1024]{2,1,0:T(2,128)(2,1)S(1)} all-to-all(bf16[16,2,1024]{2,1,0:T(2,128)(2,1)S(1)} %reshape.234), channel_id=1, replica_groups=mesh['src'=16,'rcv'=16] {'rcv'}, dimensions={0} | all-to-all | bytes 131072 | tf_op jit(solution)/shard_map/all_to_all | solution.py:90
  277.2 11.9 %reshape.235 = bf16[16384,1,2]{2,1,0:T(2,128)(2,1)} reshape(bf16[16,2,1024]{2,1,0:T(2,128)(2,1)S(1)} %all_to_all.24) | data formatting | bytes 131072
  289.1 15.4 %copy.42 = bf16[2,1,16384]{2,0,1:T(2,128)(2,1)S(1)} copy(bf16[2,1,16384]{0,1,2:T(2,128)(2,1)} %bitcast.83) | data formatting | bytes 131072 | tf_op jit(solution)/shard_map/all_to_all | solution.py:90
  304.5 1.1 stack.26
  305.6 5.1 %all-to-all-start.2 = ((bf16[16,2,16,1024]{3,2,1,0:T(8,128)(2,1)}), bf16[16,2,16,1024]{3,2,1,0:T(8,128)(2,1)S(1)}, u32[]{:S(2)}, u32[]{:S(2)}) async-start(bf16[16,2,16,1024]{3,2,1,0:T(8,128)(2,1)} %stack.26), calls=%async_computation.2 | async-start | bytes 2097152 | tf_op jit(solution)/shard_map/all_to_all | solution.py:124
  310.8 13.3 %all-to-all-done.2 = bf16[16,2,16,1024]{3,2,1,0:T(8,128)(2,1)S(1)} async-done(((bf16[16,2,16,1024]{3,2,1,0:T(8,128)(2,1)}), bf16[16,2,16,1024]{3,2,1,0:T(8,128)(2,1)S(1)}, u32[]{:S(2)}, u32[]{:S(2)}) %all-to-all-start.2) | async-done | bytes 1048608 | tf_op jit(solution)/shard_map/all_to_all | solution.py:124
  324.4 1.3 slice_bitcast_fusion.3
  325.6 2.4 fusion.32
  328.0 2.4 multiply_bitcast_fusion.3
  330.5 3.0 fusion.10
  333.5 6.2 %copy.43 = bf16[2,1024,1024]{1,2,0:T(8,128)(2,1)} copy(bf16[2,1024,1024]{2,1,0:T(8,128)(2,1)} %fusion.10) | data formatting | bytes 8388608 | tf_op jit(solution)/shard_map/convert_element_type | solution.py:138
  339.7 1.1 slice.101
  341.5 74.4 %all-gather.5.cloned.1.call-done = bf16[2,256,1024]{2,1,0:T(8,128)(2,1)} async-done(((bf16[2,16,1024]{2,1,0:T(8,128)(2,1)}), bf16[2,256,1024]{2,1,0:T(8,128)(2,1)}) %all-gather.5.cloned.1.call-update) | async-done | bytes 1048592 | tf_op jit(solution)/shard_map/all_gather | solution.py:115
  415.9 1.3 slice_bitcast_fusion.1
  417.1 2.4 fusion.36
  419.5 2.4 multiply_bitcast_fusion.1
  422.0 3.0 fusion.11
  (31 shorter events, 5.5 us)
Async XLA Ops:
  9.0 69.8 %all-to-all-start = ((bf16[2,16,1024]{2,0,1:T(2,128)(2,1)}), bf16[2,16,1024]{2,0,1:T(2,128)(2,1)S(1)}, u32[]{:S(2)}, u32[]{:S(2)}) async-start(bf16[2,16,1024]{2,0,1:T(2,128)(2,1)} %bitcast.81), calls=%async_computation | async-start | bytes 131072 | tf_op jit(solution)/shard_map/all_to_all | solution.py:88
  20.0 304.3 %all-gather.3.cloned.1.call-start = ((), (), s32[]{:S(2)}) async-start(), calls=%async_computation.3 | async-start | bytes 1114112 | tf_op jit(solution)/shard_map/all_gather | solution.py:115
  80.2 13.9 %copy-start.2 = (f32[16,1024]{1,0:T(8,128)S(1)}, f32[16,1024]{1,0:T(8,128)}, u32[]{:S(2)}) copy-start(f32[16,1024]{1,0:T(8,128)} %param.4) | copy-start | bytes 196612
  289.1 21.7 %copy-start.3 = (f32[1024]{0:T(1024)S(1)}, f32[1024]{0:T(1024)}, u32[]{:S(2)}) copy-start(f32[1024]{0:T(1024)} %param.5) | copy-start | bytes 12292
  305.6 18.5 %all-to-all-start.2 = ((bf16[16,2,16,1024]{3,2,1,0:T(8,128)(2,1)}), bf16[16,2,16,1024]{3,2,1,0:T(8,128)(2,1)S(1)}, u32[]{:S(2)}, u32[]{:S(2)}) async-start(bf16[16,2,16,1024]{3,2,1,0:T(8,128)(2,1)} %stack.26), calls=%async_computation.2 | async-start | bytes 2097152 | tf_op jit(solution)/shard_map/all_to_all | solution.py:124
  310.7 105.1 %all-gather.5.cloned.1.call-start = ((), (), s32[]{:S(2)}) async-start(), calls=%async_computation.4 | async-start | bytes 1114112 | tf_op jit(solution)/shard_map/all_gather | solution.py:115
  328.0 2.5 copy-start
  419.5 2.5 copy-start.1
Sparse Core Ops, SparseCore 0:
  28.2 80.2 all-gather.2
  341.6 74.1 all-gather.4
